TPU v7x, 128 devices: a whole 4x4x4 slice. The times are simulated.
128 devices in a mesh: patch: 8 (over x, core), proto: 16 (over z, y).
Axes of the slice: x: 4, y: 4, z: 4, core: 2. Of those that a mesh axis runs over, the one named last changes fastest.
Arguments:
- student_feats: bfloat16 [32768, 256], P(('patch', 'proto')), may hold values from -50 to 50
- teacher_feats: bfloat16 [32768, 256], P(('patch', 'proto')), may hold values from -50 to 50
- proto_weight: bfloat16 [256, 131072], P(None, 'proto'), may hold values from -4 to 4
- mask_index: int32 [4096], P(('patch', 'proto')), may hold values from 0 to 255, as said below
- row_weight: bfloat16 [4096], P(('patch', 'proto')), may hold values from 0.5 to 4
Outputs:
- grad_student: float32 [4096, 256], P(('patch', 'proto'))
- grad_proto: float32 [256, 131072], P('patch', 'proto')
- loss: float32 [], replicated
Inputs may be any that keep to these rules, and one draw needn't show every extreme that they name: `mask_index`: entries k * 32 to (k + 1) * 32 - 1 are distinct patch positions of image k, counted from that image's first patch.
All inputs are finite; a program needn't handle non-finite values.
Results may differ from a plain program's by a relative error of at most 0.0057.
Values may be sent and summed in bfloat16 or wider, within the bound.
No kernel may reach another device: no remote copies, remote signals or barrier semaphores. Data moves between devices by JAX's collectives and lax.ppermute only.
A program may use at most 128 MiB of HBM per device.

v0:
```python
import jax
import jax.numpy as jnp
from jax import lax
from jax.sharding import PartitionSpec as P

SK_ITERS = 3


eps = 1e-06
teacher_temp = 0.07
student_temp = 0.1


def unit_rows(values):
    values = values.astype(jnp.float32)
    inverse = lax.rsqrt(jnp.sum(values * values, axis=1) + eps)
    return (values * inverse[:, None], inverse)


def finish(teacher_exp, scale_rows, scale_cols, logits, exp_logits, exp_total, weights):
    codes = teacher_exp * scale_rows[:, None] * scale_cols[None, :]
    student_probs = exp_logits / exp_total[:, None]
    grad_logits = (weights[:, None] * (student_probs - codes)).astype(jnp.bfloat16)
    log_total = jnp.log(exp_total)
    loss_partial = jnp.sum(weights[:, None] * codes * (log_total[:, None] - logits))
    return (grad_logits, loss_partial)


def feature_term(grad_logits, proto_cols):
    return (
        lax.dot_general(
            grad_logits, proto_cols, (((1,), (1,)), ((), ())), preferred_element_type=jnp.float32
        )
        / student_temp
    )


def head_term(student_rows, grad_logits):
    return (
        lax.dot_general(
            student_rows, grad_logits, (((0,), (0,)), ((), ())), preferred_element_type=jnp.float32
        )
        / student_temp
    )


def on_device(student_feats, teacher_feats, proto_weight, mask_index, row_weight):
    highest = lax.Precision.HIGHEST
    unit_student, inverse_student = unit_rows(jnp.take(student_feats, mask_index, axis=0))
    unit_teacher, _ = unit_rows(jnp.take(teacher_feats, mask_index, axis=0))
    own_student = unit_student.astype(jnp.bfloat16)
    own_teacher = unit_teacher.astype(jnp.bfloat16)
    w_float = proto_weight.astype(jnp.float32)
    col_inverse = lax.rsqrt(jnp.sum(w_float * w_float, axis=0) + eps)
    unit_proto = w_float * col_inverse[None, :]
    proto_unit = unit_proto.astype(jnp.bfloat16)
    teacher_rows, student_rows, weights = (
        lax.all_gather(own_teacher, "proto", axis=0, tiled=True),
        lax.all_gather(own_student, "proto", axis=0, tiled=True),
        lax.all_gather(row_weight, "proto", axis=0, tiled=True),
    )
    weights = weights.astype(jnp.float32)
    teacher_exp = jnp.exp(
        jnp.dot(teacher_rows, proto_unit, preferred_element_type=jnp.float32) / teacher_temp
    )
    scale_rows = jnp.ones((teacher_rows.shape[0],), jnp.float32)
    for sweep in range(SK_ITERS):
        col_part = jnp.dot(scale_rows, teacher_exp, precision=highest)
        scale_cols = 1.0 / lax.psum(col_part, "patch")
        row_part = jnp.dot(teacher_exp, scale_cols, precision=highest)
        scale_rows = 1.0 / lax.psum(row_part, "proto")
    logits = jnp.dot(student_rows, proto_unit, preferred_element_type=jnp.float32) / student_temp
    exp_logits = jnp.exp(logits)
    exp_total = lax.psum(jnp.sum(exp_logits, axis=1), "proto")
    grad_logits, loss_partial = finish(
        teacher_exp, scale_rows, scale_cols, logits, exp_logits, exp_total, weights
    )
    feature_grad = lax.psum_scatter(
        feature_term(grad_logits, proto_unit), "proto", scatter_dimension=0, tiled=True
    )
    row_share = proto_unit.shape[0] // lax.axis_size("patch")
    row_offset = lax.axis_index("patch") * row_share
    head_full = lax.psum(head_term(student_rows, grad_logits), "patch")
    inner = jnp.sum(unit_proto * head_full, axis=0)
    whole_grad = col_inverse[None, :] * (head_full - unit_proto * inner[None, :])
    grad_proto = lax.dynamic_slice_in_dim(whole_grad, row_offset, row_share, 0)
    loss_total, weight_total = lax.psum(
        (loss_partial, jnp.sum(row_weight.astype(jnp.float32))), ("patch", "proto")
    )
    grad_student = inverse_student[:, None] * (
        feature_grad - unit_student * jnp.sum(unit_student * feature_grad, axis=1)[:, None]
    )
    return (grad_student, grad_proto, loss_total / weight_total)


def solution(mesh):
    in_specs = (
        P(("patch", "proto"), None),
        P(("patch", "proto"), None),
        P(None, "proto"),
        P(("patch", "proto")),
        P(("patch", "proto")),
    )
    out_specs = (P(("patch", "proto"), None), P("patch", "proto"), P())
    return jax.shard_map(
        on_device, mesh=mesh, in_specs=in_specs, out_specs=out_specs, check_vma=False
    )
```

profile of v0, /device:TPU:1, one launch (start us, length us, event | category | flops | bytes accessed | tf_op | source)
XLA Modules:
  0.0 526.8 jit_solution(3142531026962949100)
XLA Ops:
  8.0 0.0 copy-start
  8.0 0.0 reduce-scatter.2.cloned.1.call-start
  8.1 0.7 compare_select_fusion
  8.7 0.7 compare_and_fusion
  9.4 0.0 copy-done
  9.4 0.6 gather_fusion
  10.1 1.5 gather_fusion.1
  11.6 0.2 fusion.17
  11.8 0.1 fusion.13
  11.9 20.8 %all_gather.11 = bf16[512,256]{1,0:T(8,128)(2,1)S(1)} all-gather(bf16[32,256]{1,0:T(8,128)(2,1)S(1)} %get-tuple-element.15), channel_id=1, replica_groups=mesh['patch'=8,'proto'=16] {'proto'}, dimensions={0}, use_global_device_ids=true | all-gather | bytes 278528 | tf_op jit(solution)/shard_map/all_gather | solution.py:58
  32.7 3.1 fusion
  35.8 4.5 multiply_exponential_fusion
  40.3 0.0 copy-start.2
  40.3 7.9 %fusion.20 = f32[1,8192]{1,0:T(1,128)S(1)} fusion(f32[512,8192]{1,0:T(8,128)S(1)} %multiply_exponential_fusion), kind=kOutput, calls=%fused_computation.41 | convolution fusion | flops 50331648 | bytes 16809984 | tf_op jit(solution)/shard_map/dot_general | solution.py:68
  48.2 0.0 copy-done.2
  48.2 26.1 %psum.71 = f32[8192]{0:T(1024)S(1)} all-reduce(f32[8192]{0:T(1024)S(1)} %bitcast.33), channel_id=1, replica_groups=mesh['patch'=8,'proto'=16] {'patch'}, use_global_device_ids=true, to_apply=%region_5.7 | all-reduce | flops 8192 | bytes 65536 | tf_op jit(solution)/shard_map/psum | solution.py:69
  74.4 17.6 %fusion.23 = f32[1,512]{1,0:T(1,128)S(1)} fusion(f32[512,8192]{1,0:T(8,128)} %copy-done.2, f32[8192,1]{0,1:T(1,128)S(1)} %bitcast.29), kind=kOutput, calls=%fused_computation.50 | convolution fusion | flops 50331648 | bytes 16812032 | tf_op jit(solution)/shard_map/dot_general | solution.py:70
  92.0 31.0 %psum.72 = f32[512]{0:T(512)S(1)} all-reduce(f32[512]{0:T(512)S(1)} %bitcast.35), channel_id=1, replica_groups=mesh['patch'=8,'proto'=16] {'proto'}, use_global_device_ids=true, to_apply=%region_6.8 | all-reduce | flops 512 | bytes 4096 | tf_op jit(solution)/shard_map/psum | solution.py:71
  123.0 11.5 %fusion.24 = f32[1,8192]{1,0:T(1,128)S(1)} fusion(f32[512,1]{0,1:T(1,128)S(1)} %bitcast.37, f32[512,8192]{1,0:T(8,128)} %copy-done.2), kind=kOutput, calls=%fused_computation.51 | convolution fusion | flops 50331648 | bytes 16812032 | tf_op jit(solution)/shard_map/dot_general | solution.py:68
  134.5 30.9 %psum.73 = f32[8192]{0:T(1024)S(1)} all-reduce(f32[8192]{0:T(1024)S(1)} %bitcast.30), channel_id=1, replica_groups=mesh['patch'=8,'proto'=16] {'patch'}, use_global_device_ids=true, to_apply=%region_7.9 | all-reduce | flops 8192 | bytes 65536 | tf_op jit(solution)/shard_map/psum | solution.py:69
  165.4 17.6 %fusion.25 = f32[1,512]{1,0:T(1,128)S(1)} fusion(f32[512,8192]{1,0:T(8,128)} %copy-done.2, f32[8192,1]{0,1:T(1,128)S(1)} %bitcast.31), kind=kOutput, calls=%fused_computation.52 | convolution fusion | flops 50331648 | bytes 16812032 | tf_op jit(solution)/shard_map/dot_general | solution.py:70
  183.0 28.5 %psum.74 = f32[512]{0:T(512)S(1)} all-reduce(f32[512]{0:T(512)S(1)} %bitcast.36), channel_id=1, replica_groups=mesh['patch'=8,'proto'=16] {'proto'}, use_global_device_ids=true, to_apply=%region_8.10 | all-reduce | flops 512 | bytes 4096 | tf_op jit(solution)/shard_map/psum | solution.py:71
  211.5 11.5 %fusion.26 = f32[1,8192]{1,0:T(1,128)S(1)} fusion(f32[512,1]{0,1:T(1,128)S(1)} %bitcast.38, f32[512,8192]{1,0:T(8,128)} %copy-done.2), kind=kOutput, calls=%fused_computation.53 | convolution fusion | flops 50331648 | bytes 16812032 | tf_op jit(solution)/shard_map/dot_general | solution.py:68
  223.0 31.0 %psum.75 = f32[8192]{0:T(1024)S(1)} all-reduce(f32[8192]{0:T(1024)S(1)} %bitcast.32), channel_id=1, replica_groups=mesh['patch'=8,'proto'=16] {'patch'}, use_global_device_ids=true, to_apply=%region_9.11 | all-reduce | flops 8192 | bytes 65536 | tf_op jit(solution)/shard_map/psum | solution.py:69
  253.9 0.0 copy-start.3
  254.0 17.8 %fusion.27 = f32[1,512]{1,0:T(1,128)S(1)} fusion(f32[512,8192]{1,0:T(8,128)} %copy-done.2, f32[8192,1]{0,1:T(1,128)S(1)} %bitcast.28), kind=kOutput, calls=%fused_computation.54 | convolution fusion | flops 50331648 | bytes 16812032 | tf_op jit(solution)/shard_map/dot_general | solution.py:70
  271.7 17.8 %all_gather.10 = bf16[512,256]{1,0:T(8,128)(2,1)S(1)} all-gather(bf16[32,256]{1,0:T(8,128)(2,1)S(1)} %get-tuple-element.14), channel_id=1, replica_groups=mesh['patch'=8,'proto'=16] {'proto'}, dimensions={0}, use_global_device_ids=true | all-gather | bytes 278528 | tf_op jit(solution)/shard_map/all_gather | solution.py:59
  289.5 0.0 copy-done.3
  289.5 0.0 copy-start.7
  289.5 0.0 copy-start.6
  289.5 7.5 %exponential_reduce_fusion = (f32[512]{0:T(512)S(1)}, f32[512,8192]{1,0:T(8,128)}) fusion(bf16[512,256]{1,0:T(8,128)(2,1)S(1)} %all_gather.10, f32[8192]{0:T(1024)S(1)} %add_rsqrt_fusion, bf16[256,8192]{1,0:T(8,128)(2,1)S(1)} %copy-done.3), kind=kOutput, calls=%fused_computation.6 | convolution fusion | flops 2162163200 | bytes 21268480 | tf_op jit(solution)/shard_map/dot_general | solution.py:72
  297.0 30.9 %all-reduce.2 = (f32[512]{0:T(512)S(1)}, f32[512]{0:T(512)S(1)}) all-reduce(f32[512]{0:T(512)S(1)} %bitcast.34, f32[512]{0:T(512)S(1)} %get-tuple-element.16), channel_id=1, replica_groups=mesh['patch'=8,'proto'=16] {'proto'}, use_global_device_ids=true, to_apply=%region_10.12 | all-reduce | flops 1024 | bytes 8192 | tf_op jit(solution)/shard_map/psum | solution.py:71
  327.9 0.0 copy-done.7
  327.9 0.6 dynamic-slice
  329.2 0.0 copy-done.6
  329.2 0.2 dynamic-update-slice
  329.4 29.0 %all-reduce = bf16[512]{0:T(512)(128)(2,1)S(1)} all-reduce(bf16[512]{0:T(512)(128)(2,1)S(1)} %dynamic-update-slice), channel_id=1, replica_groups=mesh['patch'=8,'proto'=16] {'proto'}, use_global_device_ids=true, to_apply=%add | all-reduce | flops 512 | bytes 2048
  358.4 0.0 copy-start.4
  358.4 14.4 %multiply_reduce_fusion = (f32[]{:T(128)}, bf16[512,8192]{1,0:T(8,128)(2,1)S(1)}) fusion(f32[512,8192]{1,0:T(8,128)} %copy-done.2, f32[512,8192]{1,0:T(8,128)} %get-tuple-element.17, f32[512]{0:T(512)S(1)} %log.3, f32[8192]{0:T(1024)S(1)} %broadcast_divide_fusion, f32[512]{0:T(512)S(1)} %broadcast_divide_fusion.5, f32[512]{0:T(512)S(1)} %convert_element_type.28, ...), kind=kLoop, calls=%fused_computation.2 | loop fusion | flops 46137344 | bytes 41984004 | tf_op jit(solution)/shard_map/reduce_sum | solution.py:25
  372.9 0.0 copy-start.5
  372.9 3.2 copy-done.5
  376.1 0.0 copy-done.4
  376.1 3.2 fusion.7
  379.3 0.0 reduce-scatter.2.cloned.1.call-update
  379.3 0.0 all-reduce.5.cloned.1.call-start
  379.4 9.0 %convolution_multiply_fusion = f32[256,8192]{1,0:T(8,128)} fusion(bf16[512,256]{1,0:T(8,128)(2,1)S(1)} %all_gather.10, bf16[512,8192]{1,0:T(8,128)(2,1)} %copy-done.5), kind=kOutput, calls=%fused_computation.7 | convolution fusion | flops 2149580800 | bytes 17039360 | tf_op jit(solution)/shard_map/dot_general | solution.py:40
  388.3 0.0 all-reduce.5.cloned.1.call-update
  388.4 0.6 convert_reduce_fusion
  389.0 85.0 %all-reduce.1 = (f32[]{:T(128)}, f32[]{:T(128)}) all-reduce(f32[]{:T(128)} %get-tuple-element.10, f32[]{:T(128)} %convert_reduce_fusion), channel_id=1, replica_groups=mesh['patch'=8,'proto'=16] {'patch','proto'}, use_global_device_ids=true, to_apply=%region_16.18 | all-reduce | flops 2 | bytes 16 | tf_op jit(solution)/shard_map/psum | solution.py:87
  475.3 0.0 reduce-scatter.2.cloned.1.call-done
  475.3 0.9 fusion.14
  476.2 0.0 copy-start.1
  476.3 1.5 fusion.16
  477.8 32.0 %all-reduce.5.cloned.1.call-done = f32[256,8192]{1,0:T(8,128)} async-done(((f32[256,8192]{1,0:T(8,128)}), f32[256,8192]{1,0:T(8,128)}) %all-reduce.5.cloned.1.call-update) | async-done | bytes 8388624 | tf_op jit(solution)/shard_map/psum | solution.py:83
  509.8 6.0 %multiply_reduce_fusion.1 = (f32[8192]{0:T(1024)S(1)}, f32[256,8192]{1,0:T(8,128)S(1)}) fusion(f32[256,8192]{1,0:T(8,128)} %all-reduce.5.cloned.1.call-done, f32[8192]{0:T(1024)S(1)} %add_rsqrt_fusion, bf16[256,8192]{1,0:T(8,128)(2,1)} %param.9), kind=kLoop, calls=%fused_computation.11 | loop fusion | flops 8380416 | bytes 21037056 | tf_op jit(solution)/shard_map/reduce_sum | solution.py:84
  515.7 2.3 fusion.10
  518.1 0.0 copy-done.1
  (12 shorter events, 0.1 us)
Async XLA Ops:
  8.0 1.4 copy-start
  8.0 467.3 %reduce-scatter.2.cloned.1.call-start = ((), (), s32[]{:S(2)}) async-start(), calls=%async_computation.1 | async-start | bytes 557056 | tf_op jit(solution)/shard_map/reduce_scatter | solution.py:78
  40.3 8.0 %copy-start.2 = (f32[512,8192]{1,0:T(8,128)}, f32[512,8192]{1,0:T(8,128)S(1)}, u32[]{:S(2)}) copy-start(f32[512,8192]{1,0:T(8,128)S(1)} %multiply_exponential_fusion) | copy-start | bytes 50331652
  253.9 35.6 %copy-start.3 = (bf16[256,8192]{1,0:T(8,128)(2,1)S(1)}, bf16[256,8192]{1,0:T(8,128)(2,1)}, u32[]{:S(2)}) copy-start(bf16[256,8192]{1,0:T(8,128)(2,1)} %param.9) | copy-start | bytes 12582916
  289.5 38.4 %copy-start.7 = (u32[128]{0:T(128)S(1)}, u32[128]{0:T(128)}, u32[]{:S(2)}) copy-start(u32[128]{0:T(128)} %constant.44) | copy-start | bytes 1540
  289.5 39.6 %copy-start.6 = (bf16[32]{0:T(256)(128)(2,1)S(1)}, bf16[32]{0:T(256)(128)(2,1)}, u32[]{:S(2)}) copy-start(bf16[32]{0:T(256)(128)(2,1)} %param.11) | copy-start | bytes 196
  358.4 17.7 %copy-start.4 = (bf16[256,8192]{1,0:T(8,128)(2,1)S(1)}, bf16[256,8192]{1,0:T(8,128)(2,1)}, u32[]{:S(2)}) copy-start(bf16[256,8192]{1,0:T(8,128)(2,1)} %param.9) | copy-start | bytes 12582916
  372.9 3.2 copy-start.5
  379.3 130.5 %all-reduce.5.cloned.1.call-start = ((), (), s32[]{:S(2)}) async-start(), calls=%async_computation.2 | async-start | bytes 16777216 | tf_op jit(solution)/shard_map/psum | solution.py:83
  476.2 41.8 %copy-start.1 = (bf16[256,256]{1,0:T(8,128)(2,1)S(1)}, bf16[256,256]{1,0:T(8,128)(2,1)}, u32[]{:S(2)}) copy-start(bf16[256,256]{1,0:T(8,128)(2,1)} %param.7) | copy-start | bytes 393220
Sparse Core Ops, SparseCore 0:
  379.4 87.7 reduce-scatter.1
Sparse Core Ops, SparseCore 1:
  388.5 121.3 all-reduce.4
where the time goes:
time: 536 us; the launch traced here: 527 us
  blocking collectives  331 us (62%)
  matrix products  108 us (20%)
  waiting for transfers between devices  32.1 us (6%)
  other arithmetic  30.5 us (6%)
  between operations  18.9 us (4%)
  local copies, waits for them, and re-layouts  6.24 us (1%)
    psum x3, blocking collectives, on_device(): scale_rows = 1.0 / lax.psum(row_part, 'proto')  90.4 us
    psum x3, blocking collectives, on_device(): scale_cols = 1.0 / lax.psum(col_part, 'patch')  88 us
    psum x1, blocking collectives, on_device(): lax.psum((loss_partial, jnp.sum(row_weight.astype(jnp.float32))), ('patch...  85 us
    dot_general x3, matrix products, on_device(): row_part = jnp.dot(teacher_exp, scale_cols, precision=highest)  53 us
    psum x1, waiting for transfers between devices, on_device(): head_full = lax.psum(head_term(student_rows, grad_logits), 'patch')  32 us
    dot_general x3, matrix products, on_device(): col_part = jnp.dot(scale_rows, teacher_exp, precision=highest)  30.8 us
    unnamed x1, blocking collectives  29 us
    all_gather x1, blocking collectives, on_device(): lax.all_gather(own_teacher, 'proto', axis=0, tiled=True)  20.8 us
  transfers between devices with their start and end apart: 2, of which 1 were waited for; matrix products, arithmetic and copies ran while one was open for 2% of the time, Pallas kernels for 0%

commit v1 on v0

v1 whole, which is shorter than its diff:
```python
import functools

import jax
import jax.numpy as jnp
from jax import lax
from jax.experimental import pallas as pl
from jax.experimental.pallas import tpu as pltpu
from jax.sharding import PartitionSpec as P

SK_ITERS = 3
EPS = 1e-06
TEACHER_TEMP = 0.07
STUDENT_TEMP = 0.1
F32 = jnp.float32
BF16 = jnp.bfloat16
BLOCK = 2048
VMEM_LIMIT = 48 * 1024 * 1024

NN = (((1,), (0,)), ((), ()))
NT = (((1,), (1,)), ((), ()))


def mm(a, b, dims=NN):
    return lax.dot_general(a, b, dims, preferred_element_type=F32)


def call(body, name, out_shape, flops=0, bytes_accessed=0, **kwargs):
    return pl.pallas_call(
        body,
        name=name,
        out_shape=out_shape,
        compiler_params=pltpu.CompilerParams(vmem_limit_bytes=VMEM_LIMIT),
        cost_estimate=pl.CostEstimate(
            flops=flops, bytes_accessed=bytes_accessed, transcendentals=0
        ),
        **kwargs,
    )


def whole(shape):
    return pl.BlockSpec(shape, lambda j: (0,) * len(shape))


def cols(rows):
    return pl.BlockSpec((rows, BLOCK), lambda j: (0, j))


def shape(dims, dtype):
    return jax.ShapeDtypeStruct(dims, dtype)


def three_terms(row):
    high = row.astype(BF16).astype(F32)
    rest = row - high
    mid = rest.astype(BF16).astype(F32)
    low = rest - mid
    index = lax.broadcasted_iota(jnp.int32, (16, row.shape[1]), 0)
    terms = jnp.where(
        index == 0, high, jnp.where(index == 1, mid, jnp.where(index == 2, low, 0.0))
    )
    return terms.astype(BF16)


def rows_body(place_ref, student_ref, teacher_ref, index_ref, weight_ref, rows_ref, x_ref, w_ref):
    picks = index_ref[...]
    length = student_ref.shape[0]
    count = picks.shape[1]
    one_hot = (lax.broadcasted_iota(jnp.int32, (length, count), 0) == picks).astype(BF16)
    tn = (((0,), (0,)), ((), ()))
    x = mm(one_hot, student_ref[...], tn)
    y = mm(one_hot, teacher_ref[...], tn)
    x_ref[...] = x
    unit_x = x * lax.rsqrt(jnp.sum(x * x, axis=1, keepdims=True) + EPS)
    unit_y = y * lax.rsqrt(jnp.sum(y * y, axis=1, keepdims=True) + EPS)
    both = jnp.concatenate([unit_y.astype(BF16), unit_x.astype(BF16)], axis=0)
    rows_ref[...] = jnp.broadcast_to(both[None], rows_ref.shape)
    lanes = w_ref.shape[1]
    spot = lax.broadcasted_iota(jnp.int32, (count, lanes), 1) - place_ref[0] * count
    spread = (spot == lax.broadcasted_iota(jnp.int32, (count, lanes), 0)).astype(BF16)
    w_ref[...] = jnp.broadcast_to(mm(weight_ref[...], spread), w_ref.shape)


def proto_body(w_ref, unit_ref, inverse_ref):
    w = w_ref[...].astype(F32)
    inverse = lax.rsqrt(jnp.sum(w * w, axis=0, keepdims=True) + EPS)
    inverse_ref[...] = inverse
    unit_ref[...] = (w * inverse).astype(BF16)


def table_body(rows_ref, unit_ref, table_ref, sums_ref):
    half = rows_ref.shape[1] // 2
    teacher = rows_ref[:, :half, :].reshape(-1, rows_ref.shape[2])
    table = jnp.exp(mm(teacher, unit_ref[...]) * (1.0 / TEACHER_TEMP)).astype(BF16)
    table_ref[...] = table
    total = jnp.sum(table.astype(F32), axis=0, keepdims=True)
    sums_ref[...] = jnp.broadcast_to(total, sums_ref.shape)


def row_pass_body(sums_ref, table_ref, extra_ref, out_ref, acc_ref):
    @pl.when(pl.program_id(0) == 0)
    def _():
        acc_ref[...] = jnp.zeros_like(acc_ref)

    scale = 1.0 / jnp.sum(sums_ref[...], axis=0, keepdims=True)
    acc_ref[...] += mm(three_terms(scale), table_ref[...], NT)

    @pl.when(pl.program_id(0) == pl.num_programs(0) - 1)
    def _():
        total = jnp.sum(acc_ref[...], axis=0, keepdims=True)
        n = total.shape[1]
        out_ref[:, :n] = jnp.broadcast_to(total, (out_ref.shape[0], n))
        if out_ref.shape[1] > n:
            out_ref[:, n:] = jnp.broadcast_to(extra_ref[0:1, :], (out_ref.shape[0], n))


def col_pass_body(totals_ref, table_ref, out_ref):
    n = table_ref.shape[0]
    scale = 1.0 / jnp.sum(totals_ref[:, :n], axis=0, keepdims=True)
    total = jnp.sum(mm(three_terms(scale), table_ref[...]), axis=0, keepdims=True)
    out_ref[...] = jnp.broadcast_to(total, out_ref.shape)


def student_body(rows_ref, unit_ref, table_ref, sums_ref, feature_ref, turned_ref, acc_ref):
    half = rows_ref.shape[1] // 2
    student = rows_ref[:, half:, :].reshape(-1, rows_ref.shape[2])
    first = pl.program_id(0) == 0

    @pl.when(first)
    def _():
        acc_ref[...] = jnp.zeros_like(acc_ref)
        feature_ref[...] = jnp.zeros_like(feature_ref)
        d = student.shape[1]
        eye = (
            lax.broadcasted_iota(jnp.int32, (d, d), 0)
            == lax.broadcasted_iota(jnp.int32, (d, d), 1)
        ).astype(BF16)
        turned_ref[...] = mm(eye, student, NT).astype(BF16)

    unit = unit_ref[...]
    table = jnp.exp(mm(student, unit) * (1.0 / STUDENT_TEMP)).astype(BF16)
    table_ref[...] = table
    ones = jnp.ones((16, table.shape[1]), BF16)
    acc_ref[...] += mm(ones, table, NT)
    feature_ref[...] += mm(unit, table, NT)

    @pl.when(pl.program_id(0) == pl.num_programs(0) - 1)
    def _():
        sums_ref[...] = acc_ref[0:8, :]


def codes_feature_body(sums_ref, unit_ref, table_ref, feature_ref):
    @pl.when(pl.program_id(0) == 0)
    def _():
        feature_ref[...] = jnp.zeros_like(feature_ref)

    scale = 1.0 / jnp.sum(sums_ref[...], axis=0, keepdims=True)
    scaled = (unit_ref[...].astype(F32) * scale).astype(BF16)
    feature_ref[...] += mm(scaled, table_ref[...], NT)


def head_body(
    place_ref,
    totals_ref,
    exp_totals_ref,
    sums_ref,
    turned_ref,
    codes_ref,
    probs_ref,
    w_ref,
    inverse_ref,
    keep_ref,
    send_ref,
    grad_ref,
):
    n = codes_ref.shape[0]
    row_scale = 1.0 / jnp.sum(totals_ref[:, :n], axis=0, keepdims=True)
    exp_total = jnp.sum(exp_totals_ref[:, :n], axis=0, keepdims=True)
    weights = jnp.sum(exp_totals_ref[:, n:], axis=0, keepdims=True)
    turned = turned_ref[...].astype(F32)
    left_probs = (turned * (weights / exp_total * (1.0 / STUDENT_TEMP))).astype(BF16)
    left_codes = (turned * (weights * row_scale * (1.0 / STUDENT_TEMP))).astype(BF16)
    scale_cols = 1.0 / jnp.sum(sums_ref[...], axis=0, keepdims=True)
    head = mm(left_probs, probs_ref[...]) - scale_cols * mm(left_codes, codes_ref[...])
    inverse = inverse_ref[...]
    unit = w_ref[...].astype(F32) * inverse
    inner = jnp.sum(unit * head, axis=0, keepdims=True)
    grad = inverse * (head - unit * inner)
    grad_ref[...] = grad.reshape(grad_ref.shape)
    x = place_ref[1]
    core = place_ref[2]
    for k in range(keep_ref.shape[0]):
        keep_ref[k] = grad_ref[x ^ k, core]
        send_ref[k] = grad_ref[x ^ k, 1 - core].astype(BF16)


def feature_body(
    totals_ref, exp_totals_ref, probs_ref, codes_ref, turned_ref, out_ref, loss_ref
):
    n = probs_ref.shape[1]
    total = jnp.sum(totals_ref[:, :n], axis=0, keepdims=True)
    exp_total = jnp.sum(exp_totals_ref[:, :n], axis=0, keepdims=True)
    weights = jnp.sum(exp_totals_ref[:, n:], axis=0, keepdims=True)
    codes = codes_ref[...]
    over = weights / total * (1.0 / STUDENT_TEMP)
    feature = probs_ref[...] * (weights / exp_total * (1.0 / STUDENT_TEMP)) - codes * over
    rows = feature.T.astype(BF16)
    out_ref[...] = rows.reshape(out_ref.shape)
    share = 1.0 / out_ref.shape[0]
    cross = jnp.sum(turned_ref[...].astype(F32) * codes, axis=0, keepdims=True)
    part = jnp.sum(weights * jnp.log(exp_total) * share - over * cross)
    count = jnp.sum(weights) * share
    lane = lax.broadcasted_iota(jnp.int32, loss_ref.shape, 1)
    loss_ref[...] = jnp.where(lane == 0, part, jnp.where(lane == 1, count, 0.0))


def on_device(student_feats, teacher_feats, proto_weight, mask_index, row_weight):
    n_patch, n_proto = lax.axis_size("patch"), lax.axis_size("proto")
    d, protos = proto_weight.shape
    own = mask_index.shape[0]
    rows = own * n_proto
    steps = protos // BLOCK
    chips = n_patch // 2
    share = d // n_patch
    patch, proto = lax.axis_index("patch"), lax.axis_index("proto")
    place = jnp.stack([proto, patch // 2, patch % 2]).astype(jnp.int32)
    smem = pl.BlockSpec(memory_space=pltpu.SMEM)
    product = 2 * rows * d * protos
    table_bytes = rows * protos * 2

    def exchange(array, axis):
        return lax.all_to_all(array, axis, 0, 0, tiled=True)

    own_rows, x_rows, own_weights = call(
        rows_body,
        "own_rows",
        (
            shape((n_proto, 2 * own, d), BF16),
            shape((own, d), F32),
            shape((n_proto, rows), F32),
        ),
        flops=1 << 24,
        bytes_accessed=1 << 21,
        in_specs=[smem] + [pl.BlockSpec(memory_space=pltpu.VMEM)] * 4,
    )(place, student_feats, teacher_feats, mask_index[None, :], row_weight[None, :])

    unit, inverse = call(
        proto_body,
        "proto_unit",
        (shape((d, protos), BF16), shape((1, protos), F32)),
        flops=6 * d * protos,
        bytes_accessed=4 * d * protos,
        grid=(steps,),
        in_specs=[cols(d)],
        out_specs=[cols(d), cols(1)],
    )(proto_weight)

    all_rows = exchange(own_rows, "proto")
    rows_spec = whole((n_proto, 2 * own, d))

    codes, sums = call(
        table_body,
        "teacher_table",
        (shape((rows, protos), BF16), shape((n_patch, protos), F32)),
        flops=product,
        bytes_accessed=table_bytes,
        grid=(steps,),
        in_specs=[rows_spec, cols(d)],
        out_specs=[cols(rows), cols(n_patch)],
    )(all_rows, unit)

    probs, exp_sums, probs_feature, turned = call(
        student_body,
        "student_table",
        (
            shape((rows, protos), BF16),
            shape((8, rows), F32),
            shape((d, rows), F32),
            shape((d, rows), BF16),
        ),
        flops=2 * product,
        bytes_accessed=table_bytes,
        grid=(steps,),
        in_specs=[rows_spec, cols(d)],
        out_specs=[cols(rows), whole((8, rows)), whole((d, rows)), whole((d, rows))],
        scratch_shapes=[pltpu.VMEM((16, rows), F32)],
    )(all_rows, unit)
    exp_part = jnp.concatenate(
        [jnp.broadcast_to(exp_sums[0:1], (n_proto, rows)), own_weights], axis=1
    )
    exp_totals = exchange(exp_part, "proto")

    for sweep in range(SK_ITERS):
        all_sums = exchange(sums, "patch")
        part = call(
            row_pass_body,
            "row_pass",
            shape((n_proto, rows), F32),
            flops=product // 4,
            bytes_accessed=table_bytes,
            grid=(steps,),
            in_specs=[cols(n_patch), cols(rows), whole((8, rows))],
            out_specs=whole((n_proto, rows)),
            scratch_shapes=[pltpu.VMEM((16, rows), F32)],
        )(all_sums, codes, exp_sums)
        totals = exchange(part, "proto")
        if sweep < SK_ITERS - 1:
            sums = call(
                col_pass_body,
                "col_pass",
                shape((n_patch, protos), F32),
                flops=product // 4,
                bytes_accessed=table_bytes,
                grid=(steps,),
                in_specs=[whole((n_proto, rows)), cols(rows)],
                out_specs=cols(n_patch),
            )(totals, codes)

    codes_feature = call(
        codes_feature_body,
        "codes_feature",
        shape((d, rows), F32),
        flops=product,
        bytes_accessed=table_bytes,
        grid=(steps,),
        in_specs=[cols(n_patch), cols(d), cols(rows)],
        out_specs=whole((d, rows)),
    )(all_sums, unit, codes)

    keep, send = call(
        head_body,
        "head",
        (shape((chips, share, protos), F32), shape((chips, share, protos), BF16)),
        flops=2 * product,
        bytes_accessed=3 * table_bytes,
        grid=(steps,),
        in_specs=[
            smem,
            whole((n_proto, rows)),
            whole((n_proto, 2 * rows)),
            cols(n_patch),
            whole((d, rows)),
            cols(rows),
            cols(rows),
            cols(d),
            cols(1),
        ],
        out_specs=[
            pl.BlockSpec((chips, share, BLOCK), lambda j: (0, 0, j)),
            pl.BlockSpec((chips, share, BLOCK), lambda j: (0, 0, j)),
        ],
        scratch_shapes=[pltpu.VMEM((chips, 2, share, BLOCK), F32)],
    )(place, totals, exp_totals, all_sums, turned, codes, probs, proto_weight, inverse)

    def hop(array, bits):
        return lax.ppermute(array, "patch", [(i, i ^ bits) for i in range(n_patch)])

    near = hop(send, 1)
    grad_proto = keep[0] + near[0].astype(F32)
    for k in range(1, chips):
        pair = (keep[k] + near[k].astype(F32)).astype(BF16)
        grad_proto = grad_proto + hop(pair, 2 * k).astype(F32)

    feature_part, loss_part = call(
        feature_body,
        "feature",
        (shape((n_proto, own, d), BF16), shape((n_patch * n_proto, 128), F32)),
        flops=1 << 24,
        bytes_accessed=1 << 21,
    )(totals, exp_totals, probs_feature, codes_feature, turned)
    feature = jnp.sum(exchange(feature_part, "proto").astype(F32), axis=0)
    losses = jnp.sum(exchange(loss_part, ("patch", "proto")), axis=0)
    loss = losses[0] / losses[1]

    inverse_student = lax.rsqrt(jnp.sum(x_rows * x_rows, axis=1, keepdims=True) + EPS)
    unit_student = x_rows * inverse_student
    grad_student = inverse_student * (
        feature - unit_student * jnp.sum(unit_student * feature, axis=1, keepdims=True)
    )
    return (grad_student, grad_proto, loss)


def solution(mesh):
    both = ("patch", "proto")
    in_specs = (P(both, None), P(both, None), P(None, "proto"), P(both), P(both))
    out_specs = (P(both, None), P("patch", "proto"), P())
    return jax.shard_map(
        on_device, mesh=mesh, in_specs=in_specs, out_specs=out_specs, check_vma=False
    )
```

time: 536 us -> 215 us (0.40); the launches traced: 527 us -> 213 us
  blocking collectives: 331 us -> 30.9 us
  matrix products: 108 us -> 0 us
  Pallas kernels: 0 us -> 66.9 us
  starting transfers between devices: 0.08 us -> 43.5 us
  other arithmetic: 30.5 us -> 7.46 us
  between operations: 18.9 us -> 3.32 us
  waiting for transfers between devices: 32.1 us -> 46.5 us
  local copies, waits for them, and re-layouts: 6.24 us -> 14.2 us
    psum x7 -> x0, blocking collectives: 263 us -> none  [the longest x3 90.4 us: on_device(): scale_rows = 1.0 / lax.psum(row_part, 'proto')]
    dot_general x10 -> x0, matrix products: 108 us -> none  [the longest x3 53 us: on_device(): row_part = jnp.dot(teacher_exp, scale_cols, precision=highest)]
    pallas_call x0 -> x12, Pallas kernels: none -> 66.9 us  [the longest x3 16.1 us: on_device(): call(row_pass_body, 'row_pass', shape((n_proto, rows), F32), flops=produc...]
    all_gather x2 -> x0, blocking collectives: 38.6 us -> none  [the longest x1 20.8 us: on_device(): lax.all_gather(own_teacher, 'proto', axis=0, tiled=True)]
    all_to_all x0 -> x7, starting transfers between devices: none -> 37.5 us  [exchange(): return lax.all_to_all(array, axis, 0, 0, tiled=True)]
    psum x1 -> x0, waiting for transfers between devices: 32 us -> none  [on_device(): head_full = lax.psum(head_term(student_rows, grad_logits), 'patch')]
    all_to_all x0 -> x3, blocking collectives: none -> 30.9 us  [exchange(): return lax.all_to_all(array, axis, 0, 0, tiled=True)]
    unnamed x1 -> x0, blocking collectives: 29 us -> none
  transfers between devices with their start and end apart: 2 -> 11, of which waited for: 1 -> 7; matrix products, arithmetic and copies ran while one was open for 2% -> 3% of each run, Pallas kernels for 0% -> 12%
where the time goes in v1:
time: 215 us; the launch traced here: 213 us
  Pallas kernels  66.9 us (31%)
  waiting for transfers between devices  46.5 us (22%)
  starting transfers between devices  43.5 us (20%)
  blocking collectives  30.9 us (14%)
  local copies, waits for them, and re-layouts  14.2 us (7%)
  other arithmetic  7.46 us (3%)
  between operations  3.32 us (2%)
    all_to_all x7, starting transfers between devices, exchange(): return lax.all_to_all(array, axis, 0, 0, tiled=True)  37.5 us
    all_to_all x3, blocking collectives, exchange(): return lax.all_to_all(array, axis, 0, 0, tiled=True)  30.9 us
    all_to_all x7, waiting for transfers between devices, exchange(): return lax.all_to_all(array, axis, 0, 0, tiled=True)  26.9 us
    ppermute x4, waiting for transfers between devices, hop(): return lax.ppermute(array, 'patch', [(i, i ^ bits) for i in range(n_patch)])  19.7 us
    pallas_call x3, Pallas kernels, on_device(): call(row_pass_body, 'row_pass', shape((n_proto, rows), F32), flops=produc...  16.1 us
    pallas_call x1, Pallas kernels, on_device(): call(head_body, 'head', (shape((chips, share, protos), F32), shape((chips...  13 us
    unnamed x23, local copies, waits for them, and re-layouts  9.99 us
    pallas_call x1, Pallas kernels, on_device(): call(student_body, 'student_table', (shape((rows, protos), BF16), shape((...  9.53 us
  transfers between devices with their start and end apart: 11, of which 7 were waited for; matrix products, arithmetic and copies ran while one was open for 3% of the time, Pallas kernels for 12%

profile of v1, /device:TPU:1, one launch (start us, length us, event | category | flops | bytes accessed | tf_op | source)
XLA Modules:
  0.0 212.9 jit_solution(8272790178697935159)
XLA Ops:
  0.6 0.1 pad_add_fusion.place_ref
  0.7 0.0 copy-start.4
  0.7 0.9 copy-done.4
  1.6 0.0 copy-start.5
  1.6 0.9 copy-done.5
  2.5 0.7 copy-done.6
  3.2 0.7 copy-done.7
  3.8 1.6 own_rows.1
  5.5 8.6 %all-to-all-start = ((bf16[16,64,256]{2,1,0:T(8,128)(2,1)}), bf16[16,64,256]{2,1,0:T(8,128)(2,1)S(1)}, u32[]{:S(2)}, u32[]{:S(2)}) async-start(bf16[16,64,256]{2,1,0:T(8,128)(2,1)} %get-tuple-element.19), calls=%async_computation | async-start | bytes 1048576 | tf_op jit(solution)/shard_map/all_to_all | solution.py:231
  14.1 3.9 %proto_unit.1 = (bf16[256,8192]{1,0:T(8,128)(2,1)S(1)}, f32[1,8192]{1,0:T(1,128)S(1)}) custom-call(bf16[256,8192]{1,0:T(8,128)(2,1)} %w_ref.3), custom_call_target="tpu_custom_call" | custom-call | flops 12582912 | bytes 8388608 | tf_op jit(solution)/shard_map/proto_unit/pallas_call | solution.py:246
  18.0 0.0 copy-start
  18.0 2.0 copy-done
  20.0 4.6 %all-to-all-done.rows_ref = bf16[16,64,256]{2,1,0:T(8,128)(2,1)S(1)} async-done(((bf16[16,64,256]{2,1,0:T(8,128)(2,1)}), bf16[16,64,256]{2,1,0:T(8,128)(2,1)S(1)}, u32[]{:S(2)}, u32[]{:S(2)}) %all-to-all-start) | async-done | bytes 524320 | tf_op jit(solution)/shard_map/all_to_all | solution.py:231
  24.6 2.2 %copy-done.1 = bf16[256,8192]{1,0:T(8,128)(2,1)S(1)} copy-done((bf16[256,8192]{1,0:T(8,128)(2,1)S(1)}, bf16[256,8192]{1,0:T(8,128)(2,1)}, u32[]{:S(2)}) %copy-start.1) | copy-done | bytes 4194328
  26.8 6.4 %teacher_table.1 = (bf16[512,8192]{1,0:T(8,128)(2,1)}, f32[8,8192]{1,0:T(8,128)S(1)}) custom-call(bf16[16,64,256]{2,1,0:T(8,128)(2,1)S(1)} %all-to-all-done.rows_ref, bf16[256,8192]{1,0:T(8,128)(2,1)S(1)} %copy-done.1), custom_call_target="tpu_custom_call" | custom-call | flops 2147483648 | bytes 8388608 | tf_op jit(solution)/shard_map/teacher_table/pallas_call | solution.py:260
  33.2 1.0 copy.8
  34.2 6.2 %all-to-all-start.1 = ((f32[8,1,8192]{2,1,0:T(1,128)}), f32[8,1,8192]{2,1,0:T(1,128)S(1)}, u32[]{:S(2)}, u32[]{:S(2)}) async-start(f32[8,1,8192]{2,1,0:T(1,128)} %copy.8), calls=%async_computation.1 | async-start | bytes 524288 | tf_op jit(solution)/shard_map/all_to_all | solution.py:231
  40.4 2.2 %copy-done.2 = bf16[256,8192]{1,0:T(8,128)(2,1)S(1)} copy-done((bf16[256,8192]{1,0:T(8,128)(2,1)S(1)}, bf16[256,8192]{1,0:T(8,128)(2,1)}, u32[]{:S(2)}) %copy-start.2) | copy-done | bytes 4194328
  42.6 9.5 %student_table.1 = (bf16[512,8192]{1,0:T(8,128)(2,1)}, f32[8,512]{1,0:T(8,128)S(1)}, f32[256,512]{1,0:T(8,128)S(1)}, bf16[256,512]{1,0:T(8,128)(2,1)S(1)}) custom-call(bf16[16,64,256]{2,1,0:T(8,128)(2,1)S(1)} %all-to-all-done.rows_ref, bf16[256,8192]{1,0:T(8,128)(2,1)S(1)} %copy-done.2), custom_call_target="tpu_custom_call" | custom-call | flops 4294967296 | bytes 8388608 | tf_op jit(solution)/shard_map/student_table/pallas_call | solution.py:271
  52.1 0.0 all-to-all-done.1
  52.1 0.2 copy.32
  52.3 5.4 %row_pass.3 = f32[16,512]{1,0:T(8,128)S(1)} custom-call(f32[8,8192]{1,0:T(8,128)S(1)} %bitcast.54, bf16[512,8192]{1,0:T(8,128)(2,1)} %get-tuple-element.22.table_ref.codes_ref, f32[8,512]{1,0:T(8,128)S(1)} %get-tuple-element.23.extra_ref), custom_call_target="tpu_custom_call" | custom-call | flops 536870912 | bytes 8388608 | tf_op jit(solution)/shard_map/row_pass/pallas_call | solution.py:294
  57.7 9.1 %all_to_all.96 = f32[16,1,512]{2,1,0:T(1,128)S(1)} all-to-all(f32[16,1,512]{2,1,0:T(1,128)S(1)} %copy.9), channel_id=1, replica_groups=mesh['patch'=8,'proto'=16] {'proto'}, dimensions={0} | all-to-all | bytes 65536 | tf_op jit(solution)/shard_map/all_to_all | solution.py:231
  66.8 4.8 %col_pass.2 = f32[8,8192]{1,0:T(8,128)S(1)} custom-call(f32[16,512]{1,0:T(8,128)S(1)} %bitcast.64, bf16[512,8192]{1,0:T(8,128)(2,1)} %get-tuple-element.22.table_ref.codes_ref), custom_call_target="tpu_custom_call" | custom-call | flops 536870912 | bytes 8388608 | tf_op jit(solution)/shard_map/col_pass/pallas_call | solution.py:307
  71.6 0.3 copy.10
  71.9 12.5 %all_to_all.97 = f32[8,1,8192]{2,1,0:T(1,128)S(1)} all-to-all(f32[8,1,8192]{2,1,0:T(1,128)S(1)} %copy.10), channel_id=1, replica_groups=mesh['patch'=8,'proto'=16] {'patch'}, dimensions={0} | all-to-all | bytes 524288 | tf_op jit(solution)/shard_map/all_to_all | solution.py:231
  84.4 0.2 copy.31
  84.6 5.4 %row_pass.4 = f32[16,512]{1,0:T(8,128)S(1)} custom-call(f32[8,8192]{1,0:T(8,128)S(1)} %bitcast.56, bf16[512,8192]{1,0:T(8,128)(2,1)} %get-tuple-element.22.table_ref.codes_ref, f32[8,512]{1,0:T(8,128)S(1)} %get-tuple-element.23.extra_ref), custom_call_target="tpu_custom_call" | custom-call | flops 536870912 | bytes 8388608 | tf_op jit(solution)/shard_map/row_pass/pallas_call | solution.py:294
  90.0 9.2 %all_to_all.98 = f32[16,1,512]{2,1,0:T(1,128)S(1)} all-to-all(f32[16,1,512]{2,1,0:T(1,128)S(1)} %copy.11), channel_id=1, replica_groups=mesh['patch'=8,'proto'=16] {'proto'}, dimensions={0} | all-to-all | bytes 65536 | tf_op jit(solution)/shard_map/all_to_all | solution.py:231
  99.2 4.8 %col_pass.3 = f32[8,8192]{1,0:T(8,128)S(1)} custom-call(f32[16,512]{1,0:T(8,128)S(1)} %bitcast.66, bf16[512,8192]{1,0:T(8,128)(2,1)} %get-tuple-element.22.table_ref.codes_ref), custom_call_target="tpu_custom_call" | custom-call | flops 536870912 | bytes 8388608 | tf_op jit(solution)/shard_map/col_pass/pallas_call | solution.py:307
  104.0 1.0 copy.12
  104.9 5.8 %all-to-all-start.5 = ((f32[8,1,8192]{2,1,0:T(1,128)}), f32[8,1,8192]{2,1,0:T(1,128)S(1)}, u32[]{:S(2)}, u32[]{:S(2)}) async-start(f32[8,1,8192]{2,1,0:T(1,128)} %copy.12), calls=%async_computation.5 | async-start | bytes 524288 | tf_op jit(solution)/shard_map/all_to_all | solution.py:231
  110.8 0.7 copy.14
  111.4 5.8 %all-to-all-done.5 = f32[8,1,8192]{2,1,0:T(1,128)S(1)} async-done(((f32[8,1,8192]{2,1,0:T(1,128)}), f32[8,1,8192]{2,1,0:T(1,128)S(1)}, u32[]{:S(2)}, u32[]{:S(2)}) %all-to-all-start.5) | async-done | bytes 262176 | tf_op jit(solution)/shard_map/all_to_all | solution.py:231
  117.3 3.5 %all-to-all-start.7 = ((f32[16,1,1024]{2,1,0:T(1,128)}), f32[16,1,1024]{2,1,0:T(1,128)S(1)}, u32[]{:S(2)}, u32[]{:S(2)}) async-start(f32[16,1,1024]{2,1,0:T(1,128)} %copy.14), calls=%async_computation.7 | async-start | bytes 131072 | tf_op jit(solution)/shard_map/all_to_all | solution.py:231
  120.7 0.2 copy.30
  120.9 5.4 %row_pass.5 = f32[16,512]{1,0:T(8,128)S(1)} custom-call(f32[8,8192]{1,0:T(8,128)S(1)} %bitcast.51, bf16[512,8192]{1,0:T(8,128)(2,1)} %get-tuple-element.22.table_ref.codes_ref, f32[8,512]{1,0:T(8,128)S(1)} %get-tuple-element.23.extra_ref), custom_call_target="tpu_custom_call" | custom-call | flops 536870912 | bytes 8388608 | tf_op jit(solution)/shard_map/row_pass/pallas_call | solution.py:294
  126.3 0.6 copy.13
  126.9 0.3 all-to-all-done.7
  127.2 6.3 %all-to-all-start.6 = ((f32[16,1,512]{2,1,0:T(1,128)}), f32[16,1,512]{2,1,0:T(1,128)S(1)}, u32[]{:S(2)}, u32[]{:S(2)}) async-start(f32[16,1,512]{2,1,0:T(1,128)} %copy.13), calls=%async_computation.6 | async-start | bytes 65536 | tf_op jit(solution)/shard_map/all_to_all | solution.py:231
  133.6 6.4 %all-to-all-done.6 = f32[16,1,512]{2,1,0:T(1,128)S(1)} async-done(((f32[16,1,512]{2,1,0:T(1,128)}), f32[16,1,512]{2,1,0:T(1,128)S(1)}, u32[]{:S(2)}, u32[]{:S(2)}) %all-to-all-start.6) | async-done | bytes 32800 | tf_op jit(solution)/shard_map/all_to_all | solution.py:231
  140.0 13.0 %head.1 = (f32[4,32,8192]{2,1,0:T(8,128)}, bf16[4,32,8192]{2,1,0:T(8,128)(2,1)}) custom-call(s32[3]{0:T(128)S(1)} %pad_add_fusion.place_ref, f32[16,512]{1,0:T(8,128)S(1)} %bitcast.60, f32[16,1024]{1,0:T(8,128)S(1)} %bitcast.58, f32[8,8192]{1,0:T(8,128)S(1)} %bitcast.52, bf16[256,512]{1,0:T(8,128)(2,1)S(1)} %get-tuple-element.26.turned_ref, ...), custom_call_target="tpu_custom_call" | custom-call | flops 4294967296 | bytes 25165824 | tf_op jit(solution)/shard_map/head/pallas_call | solution.py:329
  153.0 2.8 %collective-permute-start = (bf16[4,32,8192]{2,1,0:T(8,128)(2,1)}, bf16[4,32,8192]{2,1,0:T(8,128)(2,1)S(1)}, u32[]{:S(2)}, u32[]{:S(2)}) collective-permute-start(bf16[4,32,8192]{2,1,0:T(8,128)(2,1)} %get-tuple-element.31), channel_id=1, source_target_pairs={{0,16},{16,0},{32,48},{48,32},{64,80},{80,64},{96,112},{112,96},{1... | collective-permute-start | bytes 6291464 | tf_op jit(solution)/shard_map/ppermute | solution.py:355
  155.8 0.1 multiply_reduce_fusion.1
  155.9 0.0 copy-done.3
  155.9 5.9 %codes_feature.1.codes_ref = f32[256,512]{1,0:T(8,128)S(1)} custom-call(f32[8,8192]{1,0:T(8,128)S(1)} %bitcast.53, bf16[256,8192]{1,0:T(8,128)(2,1)S(1)} %copy-done.3, bf16[512,8192]{1,0:T(8,128)(2,1)} %get-tuple-element.22.table_ref.codes_ref), custom_call_target="tpu_custom_call" | custom-call | flops 2147483648 | bytes 8388608 | tf_op jit(solution)/shard_map/codes_feature/pallas_call | solution.py:318
  161.8 1.0 feature.1
  162.8 3.5 %all-to-all-start.9 = ((f32[128,1,128]{2,1,0:T(1,128)}), f32[128,1,128]{2,1,0:T(1,128)S(1)}, u32[]{:S(2)}, u32[]{:S(2)}) async-start(f32[128,1,128]{2,1,0:T(1,128)} %bitcast.18), calls=%async_computation.9 | async-start | bytes 131072 | tf_op jit(solution)/shard_map/all_to_all | solution.py:231
  166.3 9.7 %all-to-all-done.9 = f32[128,1,128]{2,1,0:T(1,128)S(1)} async-done(((f32[128,1,128]{2,1,0:T(1,128)}), f32[128,1,128]{2,1,0:T(1,128)S(1)}, u32[]{:S(2)}, u32[]{:S(2)}) %all-to-all-start.9) | async-done | bytes 65568 | tf_op jit(solution)/shard_map/all_to_all | solution.py:231
  176.1 3.5 %all-to-all-start.8 = ((bf16[16,32,256]{2,1,0:T(8,128)(2,1)}), bf16[16,32,256]{2,1,0:T(8,128)(2,1)S(1)}, u32[]{:S(2)}, u32[]{:S(2)}) async-start(bf16[16,32,256]{2,1,0:T(8,128)(2,1)} %get-tuple-element.27), calls=%async_computation.8 | async-start | bytes 524288 | tf_op jit(solution)/shard_map/all_to_all | solution.py:231
  179.6 0.2 reduce_sum.39
  179.7 0.0 collective-permute-done
  179.7 3.2 %fusion.2 = (bf16[32,8192]{1,0:T(8,128)(2,1)S(1)}, bf16[32,8192]{1,0:T(8,128)(2,1)}, bf16[32,8192]{1,0:T(8,128)(2,1)}) fusion(f32[4,32,8192]{2,1,0:T(8,128)} %get-tuple-element.30, bf16[4,32,8192]{2,1,0:T(8,128)(2,1)S(1)} %collective-permute-done), kind=kLoop, calls=%fused_computation.6 | loop fusion | flops 2359296 | bytes 6291456 | tf_op jit(solution)/shard_map/convert_element_type | solution.py:360
  183.0 0.9 collective-permute-start.3
  183.8 1.2 collective-permute-start.2
  185.1 1.2 collective-permute-start.1
  186.2 0.6 fusion.5
  188.2 0.0 all-to-all-done.8
  188.2 0.2 multiply_reduce_fusion
  188.4 0.7 subtract_multiply_fusion
  189.1 19.3 %collective-permute-done.3 = bf16[32,8192]{1,0:T(8,128)(2,1)} collective-permute-done((bf16[32,8192]{1,0:T(8,128)(2,1)}, bf16[32,8192]{1,0:T(8,128)(2,1)}, u32[]{:S(2)}, u32[]{:S(2)}) %collective-permute-start.3) | collective-permute-done | bytes 524320 | tf_op jit(solution)/shard_map/ppermute | solution.py:355
  208.4 0.0 collective-permute-done.2
  208.4 0.3 collective-permute-done.1
  208.8 3.0 %fusion.1 = f32[32,8192]{1,0:T(8,128)} fusion(bf16[32,8192]{1,0:T(8,128)(2,1)} %collective-permute-done.3, bf16[32,8192]{1,0:T(8,128)(2,1)} %collective-permute-done.2, bf16[32,8192]{1,0:T(8,128)(2,1)} %collective-permute-done.1, f32[4,32,8192]{2,1,0:T(8,128)} %get-tuple-element.30, bf16[4,32,8192]{2,1,0:T(8,128)(2,1)S(1)} %collective-permute-done), kind=kLoop, calls=%fused_computation.2 | loop fusion | flops 2097152 | bytes 4194304 | tf_op jit(solution)/shard_map/add | solution.py:361
  (16 shorter events, 0.2 us)
Async XLA Ops:
  0.7 0.9 copy-start.4
  1.6 0.9 copy-start.5
  2.5 0.7 copy-start.6
  3.2 0.7 copy-start.7
  5.5 19.1 %all-to-all-start = ((bf16[16,64,256]{2,1,0:T(8,128)(2,1)}), bf16[16,64,256]{2,1,0:T(8,128)(2,1)S(1)}, u32[]{:S(2)}, u32[]{:S(2)}) async-start(bf16[16,64,256]{2,1,0:T(8,128)(2,1)} %get-tuple-element.19), calls=%async_computation | async-start | bytes 1048576 | tf_op jit(solution)/shard_map/all_to_all | solution.py:231
  18.0 2.0 copy-start
  24.6 2.2 %copy-start.1 = (bf16[256,8192]{1,0:T(8,128)(2,1)S(1)}, bf16[256,8192]{1,0:T(8,128)(2,1)}, u32[]{:S(2)}) copy-start(bf16[256,8192]{1,0:T(8,128)(2,1)} %copy-done) | copy-start | bytes 12582916
  34.2 18.0 %all-to-all-start.1 = ((f32[8,1,8192]{2,1,0:T(1,128)}), f32[8,1,8192]{2,1,0:T(1,128)S(1)}, u32[]{:S(2)}, u32[]{:S(2)}) async-start(f32[8,1,8192]{2,1,0:T(1,128)} %copy.8), calls=%async_computation.1 | async-start | bytes 524288 | tf_op jit(solution)/shard_map/all_to_all | solution.py:231
  40.4 2.2 %copy-start.2 = (bf16[256,8192]{1,0:T(8,128)(2,1)S(1)}, bf16[256,8192]{1,0:T(8,128)(2,1)}, u32[]{:S(2)}) copy-start(bf16[256,8192]{1,0:T(8,128)(2,1)} %copy-done) | copy-start | bytes 12582916
  104.9 12.3 %all-to-all-start.5 = ((f32[8,1,8192]{2,1,0:T(1,128)}), f32[8,1,8192]{2,1,0:T(1,128)S(1)}, u32[]{:S(2)}, u32[]{:S(2)}) async-start(f32[8,1,8192]{2,1,0:T(1,128)} %copy.12), calls=%async_computation.5 | async-start | bytes 524288 | tf_op jit(solution)/shard_map/all_to_all | solution.py:231
  117.3 9.9 %all-to-all-start.7 = ((f32[16,1,1024]{2,1,0:T(1,128)}), f32[16,1,1024]{2,1,0:T(1,128)S(1)}, u32[]{:S(2)}, u32[]{:S(2)}) async-start(f32[16,1,1024]{2,1,0:T(1,128)} %copy.14), calls=%async_computation.7 | async-start | bytes 131072 | tf_op jit(solution)/shard_map/all_to_all | solution.py:231
  127.2 12.8 %all-to-all-start.6 = ((f32[16,1,512]{2,1,0:T(1,128)}), f32[16,1,512]{2,1,0:T(1,128)S(1)}, u32[]{:S(2)}, u32[]{:S(2)}) async-start(f32[16,1,512]{2,1,0:T(1,128)} %copy.13), calls=%async_computation.6 | async-start | bytes 65536 | tf_op jit(solution)/shard_map/all_to_all | solution.py:231
  140.0 15.9 %copy-start.3 = (bf16[256,8192]{1,0:T(8,128)(2,1)S(1)}, bf16[256,8192]{1,0:T(8,128)(2,1)}, u32[]{:S(2)}) copy-start(bf16[256,8192]{1,0:T(8,128)(2,1)} %copy-done) | copy-start | bytes 12582916
  153.0 26.7 %collective-permute-start = (bf16[4,32,8192]{2,1,0:T(8,128)(2,1)}, bf16[4,32,8192]{2,1,0:T(8,128)(2,1)S(1)}, u32[]{:S(2)}, u32[]{:S(2)}) collective-permute-start(bf16[4,32,8192]{2,1,0:T(8,128)(2,1)} %get-tuple-element.31), channel_id=1, source_target_pairs={{0,16},{16,0},{32,48},{48,32},{64,80},{80,64},{96,112},{112,96},{1... | collective-permute-start | bytes 6291464 | tf_op jit(solution)/shard_map/ppermute | solution.py:355
  162.8 13.2 %all-to-all-start.9 = ((f32[128,1,128]{2,1,0:T(1,128)}), f32[128,1,128]{2,1,0:T(1,128)S(1)}, u32[]{:S(2)}, u32[]{:S(2)}) async-start(f32[128,1,128]{2,1,0:T(1,128)} %bitcast.18), calls=%async_computation.9 | async-start | bytes 131072 | tf_op jit(solution)/shard_map/all_to_all | solution.py:231
  176.1 12.1 %all-to-all-start.8 = ((bf16[16,32,256]{2,1,0:T(8,128)(2,1)}), bf16[16,32,256]{2,1,0:T(8,128)(2,1)S(1)}, u32[]{:S(2)}, u32[]{:S(2)}) async-start(bf16[16,32,256]{2,1,0:T(8,128)(2,1)} %get-tuple-element.27), calls=%async_computation.8 | async-start | bytes 524288 | tf_op jit(solution)/shard_map/all_to_all | solution.py:231
  183.0 25.5 %collective-permute-start.3 = (bf16[32,8192]{1,0:T(8,128)(2,1)}, bf16[32,8192]{1,0:T(8,128)(2,1)}, u32[]{:S(2)}, u32[]{:S(2)}) collective-permute-start(bf16[32,8192]{1,0:T(8,128)(2,1)} %get-tuple-element.34), channel_id=1, source_target_pairs={{0,96},{16,112},{32,64},{48,80},{64,32},{80,48},{96,0},{112,16},{1... | collective-permute-start | bytes 1572872 | tf_op jit(solution)/shard_map/ppermute | solution.py:355
  183.8 24.6 %collective-permute-start.2 = (bf16[32,8192]{1,0:T(8,128)(2,1)}, bf16[32,8192]{1,0:T(8,128)(2,1)}, u32[]{:S(2)}, u32[]{:S(2)}) collective-permute-start(bf16[32,8192]{1,0:T(8,128)(2,1)} %get-tuple-element.35), channel_id=1, source_target_pairs={{0,64},{16,80},{32,96},{48,112},{64,0},{80,16},{96,32},{112,48},{1... | collective-permute-start | bytes 1572872 | tf_op jit(solution)/shard_map/ppermute | solution.py:355
  185.1 23.7 %collective-permute-start.1 = (bf16[32,8192]{1,0:T(8,128)(2,1)S(1)}, bf16[32,8192]{1,0:T(8,128)(2,1)}, u32[]{:S(2)}, u32[]{:S(2)}) collective-permute-start(bf16[32,8192]{1,0:T(8,128)(2,1)S(1)} %get-tuple-element.33), channel_id=1, source_target_pairs={{0,32},{16,48},{32,0},{48,16},{64,96},{80,112},{96,64},{112,80},{1... | collective-permute-start | bytes 1572872 | tf_op jit(solution)/shard_map/ppermute | solution.py:355
